TPU v7x, 256 devices: a whole 4x4x8 slice. The times are simulated.
256 devices in a mesh: section: 16 (over y_hi, x, core), expert: 16 (over z, y_lo).
Axes of the slice: x: 4, y: 4 (y_hi: 2, y_lo: 2; y = y_hi * 2 + y_lo), z: 8, core: 2. Of those that a mesh axis runs over, the one named last changes fastest.
Arguments:
- cotangent: bfloat16 [16, 2048, 4096], P('section', 'expert'), may hold values from -6 to 6
- routes: int32 [16, 2048, 2], P('section', 'expert'), may hold values from 0 to 15, all different within a row; in each aligned block of 64 rows (0 to 63, 64 to 127, ..., all dimensions but the last counted through in order) at most 16 rows name the same one
- gate_prob: float32 [16, 2048, 2], P('section', 'expert'), may hold values from 0.05 to 1
- hidden: bfloat16 [16, 16, 2, 16, 16, 1536], P('section', 'expert'), may hold values from -6 to 6
Outputs:
- grad_pair: bfloat16 [8, 16, 1536, 4096], P(None, 'expert', 'section')
Inputs may be any that keep to these rules, and one draw needn't show every extreme that they name: `routes`: each row names 2 different experts. In each aligned block of 64 rows (one micro-batch of one device) no expert is named by more than 16 rows.
All inputs are finite; a program needn't handle non-finite values.
Results may differ from a plain program's by a relative error of at most 0.0059.
Values may be sent and summed in bfloat16 or wider, within the bound.
A program may use at most 128 MiB of HBM per device.

v0:
```python
from functools import partial

import jax
import jax.numpy as jnp
from jax import lax
from jax.sharding import PartitionSpec as P


def slot_index(route_blk, experts_total):
    labels = jnp.arange(experts_total, dtype=jnp.int32)
    hits = (route_blk[:, :, None] == labels).astype(jnp.int32)
    per_token = jnp.sum(hits, axis=1)
    before = jnp.cumsum(per_token, axis=0) - per_token
    return jnp.sum(hits * before[:, None, :], axis=2)


def pack_block(cot_blk, route_blk, prob_blk, experts_total, capacity):
    width = cot_blk.shape[1]
    slots = slot_index(route_blk, experts_total)
    flat = (route_blk * capacity + slots).reshape(-1)
    weighted = (prob_blk[:, :, None] * cot_blk[:, None, :].astype(jnp.float32)).astype(jnp.bfloat16)
    empty = jnp.zeros((experts_total * capacity, width), jnp.bfloat16)
    return empty.at[flat].set(weighted.reshape(-1, width)).reshape(experts_total, capacity, width)


def rows_product(acts, arrived):
    return lax.dot_general(
        acts, arrived, (((0,), (0,)), ((), ())), preferred_element_type=jnp.float32
    )


def pair_add(pieces, half):
    lower = pieces[:half].astype(jnp.float32)
    upper = jnp.flip(pieces[half:], 0).astype(jnp.float32)
    return (lower + upper).astype(jnp.bfloat16)


def local(cotangent, routes, gate_prob, hidden):
    n_section = lax.axis_size("section")
    half = n_section // 2
    mb_count = hidden.shape[2]
    sources = hidden.shape[3]
    capacity = hidden.shape[4]
    ff_width = hidden.shape[5]
    width = cotangent.shape[2]
    top_count = routes.shape[2]
    tok_block = cotangent.shape[1] // mb_count
    cot_blocks = cotangent.reshape(mb_count, tok_block, width)
    route_blocks = routes.reshape(mb_count, tok_block, top_count)
    prob_blocks = gate_prob.reshape(mb_count, tok_block, top_count)
    packer = partial(pack_block, experts_total=sources, capacity=capacity)
    packed = jax.vmap(packer)(cot_blocks, route_blocks, prob_blocks)
    acts = hidden.reshape(mb_count * sources * capacity, ff_width)
    arrived = lax.all_to_all(packed, "expert", split_axis=1, concat_axis=1, tiled=True)
    rows = arrived.reshape(mb_count * sources * capacity, width)
    part = rows_product(acts, rows).astype(jnp.bfloat16)
    pieces = lax.all_to_all(part[None], "section", split_axis=1, concat_axis=0, tiled=True)
    result = pair_add(pieces, half)
    return result[:, None]


def solution(mesh):
    return jax.shard_map(
        local,
        mesh=mesh,
        in_specs=(
            P("section", "expert", None),
            P("section", "expert", None),
            P("section", "expert", None),
            P("section", "expert", None, None, None, None),
        ),
        out_specs=P(None, "expert", "section", None),
        check_vma=False,
    )
```

profile of v0, /device:TPU:1, one launch (start us, length us, event | category | flops | bytes accessed | tf_op | source)
XLA Modules:
  0.0 581.9 jit_solution(12022639161730682039)
XLA Ops:
  0.0 0.9 eq.15
  0.9 0.7 broadcast_multiply_fusion
  2.0 0.1 reduce_sum.22
  2.2 0.1 mul.45
  2.4 5.3 mul.50
  7.7 6.1 %mul.51 = f32[2,128,4096]{2,1,0:T(8,128)} reshape(f32[2,64,2,4096]{3,2,1,0:T(2,128)} %mul.50) | data formatting | bytes 8388608 | tf_op jit(solution)/shard_map/vmap()/mul | solution.py:21
  14.1 4.0 multiply_convert_fusion
  18.1 2.5 broadcast_in_dim.12
  20.6 66.4 %scatter_fusion = bf16[2,256,4096]{2,1,0:T(8,128)(2,1)} fusion(bf16[2,256,4096]{2,1,0:T(8,128)(2,1)} %broadcast_in_dim.12, s32[256]{0:T(256)S(1)} %fusion.5, bf16[256,4096]{1,0:T(8,128)(2,1)} %bitcast.36), kind=kCustom, calls=%fused_computation | custom fusion | bytes 6293504 | tf_op jit(solution)/shard_map/vmap()/scatter | solution.py:23
  87.0 2.5 copy.35
  89.5 104.4 %all_to_all.17 = bf16[2,16,16,4096]{3,2,0,1:T(8,128)(2,1)S(1)} all-to-all(bf16[2,16,16,4096]{3,2,0,1:T(8,128)(2,1)S(1)} %copy.35), channel_id=1, replica_groups=mesh['section'=16,'expert'=16] {'expert'}, dimensions={1} | all-to-all | bytes 8388608 | tf_op jit(solution)/shard_map/all_to_all | solution.py:54
  193.8 0.5 copy.36
  194.4 9.7 %fusion = bf16[1,1536,4096]{1,2,0:T(8,128)(2,1)} fusion(bf16[512,4096]{1,0:T(8,128)(2,1)S(1)} %bitcast.37, bf16[512,1536]{1,0:T(8,128)(2,1)S(1)} %bitcast.29), kind=kOutput, calls=%fused_computation.2 | convolution fusion | flops 6448742400 | bytes 18350080 | tf_op jit(solution)/shard_map/dot_general | solution.py:27
  204.1 54.3 %copy.37 = bf16[1,1536,4096]{2,0,1:T(2,128)(2,1)} copy(bf16[1,1536,4096]{1,2,0:T(8,128)(2,1)} %fusion) | data formatting | bytes 25165824 | tf_op jit(solution)/shard_map/broadcast_in_dim | solution.py:57
  258.3 0.5 broadcast.51
  258.8 77.6 %reduce = bf16[1536,4096]{1,0:T(8,128)(2,1)} reduce(bf16[1536,1,4096]{2,1,0:T(2,128)(2,1)} %bitcast.33, bf16[]{:T(256)} %broadcast.51), dimensions={1}, to_apply=%bitcast.25.reduce_sub_computation | reduce | bytes 25165826
  336.4 17.6 %reshape.86 = bf16[16,2,196608]{2,1,0:T(2,128)(2,1)} reshape(bf16[1536,4096]{1,0:T(8,128)(2,1)} %reduce) | data formatting | bytes 25165824
  354.0 149.1 %all_to_all.18 = bf16[16,2,196608]{2,1,0:T(2,128)(2,1)} all-to-all(bf16[16,2,196608]{2,1,0:T(2,128)(2,1)} %reshape.86), channel_id=1, replica_groups=mesh['section'=16,'expert'=16] {'section'}, dimensions={0} | all-to-all | bytes 25165824 | tf_op jit(solution)/shard_map/all_to_all | solution.py:57
  503.1 20.6 %reshape.87 = bf16[1536,1,4096]{2,1,0:T(2,128)(2,1)} reshape(bf16[16,2,196608]{2,1,0:T(2,128)(2,1)} %all_to_all.18) | data formatting | bytes 25165824
  523.7 15.5 %slice.16 = bf16[1,768,4096]{2,0,1:T(2,128)(2,1)} slice(bf16[1,1536,4096]{2,0,1:T(2,128)(2,1)} %bitcast.30), slice={[0:1], [768:1536], [0:4096]} | slice | bytes 12582912 | tf_op jit(solution)/shard_map/slice | solution.py:34
  539.2 0.7 copy-done.2
  539.9 17.1 %copy.40 = bf16[1,1536,4096]{2,1,0:T(8,128)(2,1)} copy(bf16[1,1536,4096]{2,0,1:T(2,128)(2,1)S(1)} %bitcast.31) | data formatting | bytes 25165824
  557.0 14.4 %copy.41 = bf16[1,768,4096]{2,1,0:T(8,128)(2,1)} copy(bf16[1,768,4096]{2,0,1:T(2,128)(2,1)} %slice.16) | data formatting | bytes 12582912
  571.4 10.5 %fusion.2 = bf16[8,1,96,4096]{3,2,1,0:T(8,128)(2,1)} fusion(bf16[1,16,96,4096]{3,2,1,0:T(8,128)(2,1)} %bitcast.34, bf16[8,96,4096]{2,1,0:T(8,128)(2,1)} %bitcast.35), kind=kLoop, calls=%fused_computation.5 | loop fusion | flops 12582912 | bytes 18874368 | tf_op jit(solution)/shard_map/broadcast_in_dim | solution.py:59
  (19 shorter events, 0.8 us)
Async XLA Ops:
  0.0 194.3 %copy-start = (bf16[1,1,2,16,16,1536]{5,4,3,2,1,0:T(8,128)(2,1)S(1)}, bf16[1,1,2,16,16,1536]{5,4,3,2,1,0:T(8,128)(2,1)}, u32[]{:S(2)}) copy-start(bf16[1,1,2,16,16,1536]{5,4,3,2,1,0:T(8,128)(2,1)} %param.7) | copy-start | bytes 4718596
  7.7 6.1 %copy-start.3 = (f32[1,128,2]{1,2,0:T(2,128)S(1)}, f32[1,128,2]{1,2,0:T(2,128)}, u32[]{:S(2)}) copy-start(f32[1,128,2]{1,2,0:T(2,128)} %param.6) | copy-start | bytes 3076
  523.7 16.2 %copy-start.2 = (bf16[1536,1,4096]{2,1,0:T(2,128)(2,1)S(1)}, bf16[1536,1,4096]{2,1,0:T(2,128)(2,1)}, u32[]{:S(2)}) copy-start(bf16[1536,1,4096]{2,1,0:T(2,128)(2,1)} %reshape.87) | copy-start | bytes 37748740
  571.4 10.6 %copy-start.1 = (bf16[1,1,2,16,16,1536]{5,4,3,2,1,0:T(8,128)(2,1)S(1)}, bf16[1,1,2,16,16,1536]{5,4,3,2,1,0:T(8,128)(2,1)}, u32[]{:S(2)}) copy-start(bf16[1,1,2,16,16,1536]{5,4,3,2,1,0:T(8,128)(2,1)} %param.7) | copy-start | bytes 4718596
where the time goes:
time: 585 us; the launch traced here: 582 us
  blocking collectives  253 us (43%)
  local copies, waits for them, and re-layouts  226 us (39%)
  other arithmetic  93 us (16%)
  matrix products  9.71 us (2%)
    all_to_all x1, blocking collectives, local(): lax.all_to_all(part[None], 'section', split_axis=1, concat_axis=0, tiled=...  149 us
    all_to_all x1, blocking collectives, local(): lax.all_to_all(packed, 'expert', split_axis=1, concat_axis=1, tiled=True)  104 us
    unnamed x1, other arithmetic  77.6 us
    unnamed x14, local copies, waits for them, and re-layouts  71 us
    scatter x1, local copies, waits for them, and re-layouts, pack_block(): empty.at[flat].set(weighted.reshape(-1, width))  66.4 us
    broadcast_in_dim x1, local copies, waits for them, and re-layouts, local(): part[None]  54.3 us
    slice x1, local copies, waits for them, and re-layouts, pair_add(): upper = jnp.flip(pieces[half:], 0).astype(jnp.float32)  15.5 us

commit v1 on v0

v1 whole, which is shorter than its diff:
```python
import functools

import jax
import jax.numpy as jnp
from jax import lax
from jax.experimental import pallas as pl
from jax.experimental.pallas import tpu as pltpu
from jax.sharding import PartitionSpec as P

MESH = pl.DeviceIdType.MESH
NZ = 8
CAP = 16
TOK = 128
BLK = 64
SECTIONS = 16
AHEAD = 4
CHUNK = 256
STEPS = (
    (0, 1, 0), (1, 0, 0), (0, 3, 1), (1, 2, 0), (0, 2, 0), (1, 1, 1), (0, 0, 1), (1, 3, 0),
    (0, 1, 1), (1, 0, 1), (0, 3, 0), (1, 2, 1), (0, 2, 1), (1, 1, 0), (1, 3, 1),
)
Z_STEPS = (4, 3, 5, 2, 6, 1, 7)


def drain(ref, sem):
    pltpu.make_async_copy(ref, ref, sem).wait()


def kernel(
    cot, routes, gates, hid, out,
    cotb, rts, gts, sel, gain, packed, arrived, acts, acts_t, result,
    meta_send, meta_recv, cot_send, cot_recv, hid_send, hid_recv, z_send, z_recv, z_own, out_send, out_recv, out_own,
):
    chunks, _, _, width = cotb.shape
    ff = acts.shape[2]
    rows = result.shape[2]
    half = chunks * width
    depth = 2 * acts.shape[1]
    s = lax.axis_index("section")
    e = lax.axis_index("expert")
    y_hi, x, core = s // 8, (s // 2) % 4, s % 2
    z, y_lo = e // 2, e % 2
    chip = s // 2
    base = 2 * chip * (1 - core) + (14 - 2 * chip) * core
    pair = 2 * chip * (1 - chip // 4) + (15 - 2 * chip) * (chip // 4)
    other_e = z * 2 + 1 - y_lo
    partner = 2 * chip + 1 - core
    source = core * 2 + y_lo

    def section_at(step):
        a, b, c = step
        return ((y_hi + a) % 2) * 8 + ((x + b) % 4) * 2 + (core + c) % 2

    barrier = pltpu.get_barrier_semaphore()
    peers = [(section_at(step), e) for step in STEPS]
    peers += [(s, ((z + i) % NZ) * 2 + y_lo) for i in range(1, NZ)]
    peers += [(2 * chip, other_e), (2 * chip + 1, other_e), (14 - 2 * chip, other_e), (15 - 2 * chip, other_e)]
    for peer in peers:
        pl.semaphore_signal(barrier, inc=1, device_id=peer, device_id_type=MESH)
    pl.semaphore_wait(barrier, len(peers))

    def remote(src, dst, send, recv, device):
        pltpu.make_async_remote_copy(
            src_ref=src, dst_ref=dst, send_sem=send, recv_sem=recv, device_id=device, device_id_type=MESH
        ).start()

    targets = [(h, f, (base + h, z * 2 + (y_lo + f) % 2)) for h in range(2) for f in range(2)]

    def each_target(to_other, to_self):
        for i, (h, f, device) in enumerate(targets):
            if i == 0:
                @pl.when(core == 0)
                def _():
                    to_self(h)

                @pl.when(core == 1)
                def _():
                    to_other(i, h, device)
            else:
                to_other(i, h, device)

    def send_meta(i, h, device):
        remote(routes, rts.at[source], meta_send.at[i, 0], meta_recv.at[source, 0], device)
        remote(gates, gts.at[source], meta_send.at[i, 1], meta_recv.at[source, 1], device)

    def keep_meta(h):
        pltpu.make_async_copy(routes, rts.at[source], meta_recv.at[source, 0]).start()
        pltpu.make_async_copy(gates, gts.at[source], meta_recv.at[source, 1]).start()

    def send_rows(n):
        def cut(h):
            return cot.at[:, pl.ds(pl.multiple_of(h * half + n * width, width), width)]

        each_target(
            lambda i, h, device: remote(
                cut(h), cotb.at[n, source], cot_send.at[i], cot_recv.at[n, source], device
            ),
            lambda h: pltpu.make_async_copy(cut(h), cotb.at[n, source], cot_recv.at[n, source]).start(),
        )

    each_target(send_meta, keep_meta)
    send_rows(0)
    send_rows(1)

    block = acts.shape[1] // 2

    @pl.when(core == 0)
    def _():
        pltpu.make_async_copy(hid, acts.at[0], hid_recv.at[0]).start()
        remote(hid, acts.at[0], hid_send.at[0], hid_recv.at[0], (partner, e))

    @pl.when(core == 1)
    def _():
        for b in range(2):
            part = pl.ds(b * block, block)
            remote(hid.at[part], acts.at[1, part], hid_send.at[b], hid_recv.at[1], (base + b, e))

    def rest(n, carry):
        send_rows(n)
        return carry

    lax.fori_loop(2, chunks, rest, 0)

    token = lax.broadcasted_iota(jnp.int32, (TOK, TOK), 1)
    row = lax.broadcasted_iota(jnp.int32, (TOK, TOK), 0)
    earlier = jnp.where((row < token) & ((row >> 6) == (token >> 6)), 1.0, 0.0).astype(jnp.bfloat16)
    place = (row & (CAP - 1)).astype(jnp.float32)
    named = lax.broadcasted_iota(jnp.int32, (NZ, TOK), 0) * 2 + y_lo

    def spread(a):
        return jnp.broadcast_to(a[:, None, :], (NZ, CAP, TOK)).reshape(NZ * CAP, TOK)

    for q in range(4):
        drain(rts.at[q], meta_recv.at[q, 0])
        drain(gts.at[q], meta_recv.at[q, 1])
        first = rts[q, 0:1, :] == named
        second = rts[q, 1:2, :] == named
        hits = jnp.where(first | second, 1.0, 0.0)
        weight = jnp.where(first, gts[q, 0:1, :], 0.0) + jnp.where(second, gts[q, 1:2, :], 0.0)
        before = jnp.dot(hits.astype(jnp.bfloat16), earlier, preferred_element_type=jnp.float32)
        chosen = (spread(hits) > 0.5) & (spread(before) == place)
        weight = spread(weight)
        for b in range(2):
            mine = chosen & ((token >> 6) == b)
            sel[q, b * TOK : (b + 1) * TOK, :] = jnp.where(mine, 1.0, 0.0).astype(jnp.bfloat16)
            total = jnp.sum(jnp.where(mine, weight, 0.0), axis=1, keepdims=True)
            gain[q, b * TOK : (b + 1) * TOK, :] = jnp.broadcast_to(total, (TOK, TOK))

    def pack(n):
        for q in range(4):
            drain(cotb.at[n, q], cot_recv.at[n, q])
            picked = jnp.dot(sel[q], cotb[n, q], preferred_element_type=jnp.float32)
            scale = jnp.concatenate([gain[q]] * (width // TOK), axis=1)
            slots = (picked * scale).astype(jnp.bfloat16).reshape(2, NZ, CAP, width)
            for b in range(2):
                packed[n, :, q // 2, b, (q % 2) * CAP : (q % 2 + 1) * CAP, :] = slots[b]
        for i in Z_STEPS:
            to = (z + i) % NZ
            remote(packed.at[n, to], arrived.at[n, :, :, z], z_send, z_recv.at[n], (s, to * 2 + y_lo))
        pltpu.make_async_copy(packed.at[n, z], arrived.at[n, :, :, z], z_own.at[n]).start()

    def pack_step(n, carry):
        pack(n)
        return carry

    lax.fori_loop(0, AHEAD, pack_step, 0)

    mine = pl.ds(pl.multiple_of(core * block, block), block)
    theirs = pl.ds(pl.multiple_of((1 - core) * block, block), block)
    drain(acts.at[1, mine], hid_recv.at[1])
    remote(acts.at[1, mine], acts.at[1, mine], hid_send.at[2], hid_recv.at[2], (partner, e))
    drain(acts.at[0], hid_recv.at[0])
    drain(acts.at[1, theirs], hid_recv.at[2])

    def turn(j, carry):
        cols = pl.ds(pl.multiple_of(j * 256, 256), 256)
        for sec in range(2):
            acts_t[cols, sec * (depth // 2) : (sec + 1) * (depth // 2)] = acts[sec, :, cols].T
        return carry

    lax.fori_loop(0, ff // 256, turn, 0)

    def multiply(n, carry):
        @pl.when(n + AHEAD < chunks)
        def _():
            pack(n + AHEAD)

        drain(arrived.at[n, :, :, pl.ds(0, NZ - 1)], z_recv.at[n])
        drain(packed.at[n, 0], z_own.at[n])

        def rows_of(g, inner):
            lhs = acts_t[pl.ds(pl.multiple_of(g * 4 * rows, 4 * rows), 4 * rows), :]
            rhs = arrived[n].reshape(depth, width)
            total = jnp.dot(lhs, rhs, preferred_element_type=jnp.float32)
            result[n, pl.ds(g * 4, 4)] = total.astype(jnp.bfloat16).reshape(4, rows, width)
            return inner

        lax.fori_loop(0, SECTIONS // 4, rows_of, 0)
        place_out = out.at[pair, :, pl.ds(pl.multiple_of(core * half + n * width, width), width)]
        for step in STEPS:
            to = section_at(step)
            remote(result.at[n, to], place_out, out_send, out_recv, (to, e))
        pltpu.make_async_copy(result.at[n, s], place_out, out_own).start()
        return carry

    lax.fori_loop(0, chunks, multiply, 0)

    for i in range(4):
        if i == 0:
            @pl.when(core == 1)
            def _():
                drain(rts.at[0], meta_send.at[0, 0])
                drain(gts.at[0], meta_send.at[0, 1])
                drain(cotb.at[:, 0], cot_send.at[0])
        else:
            drain(rts.at[0], meta_send.at[i, 0])
            drain(gts.at[0], meta_send.at[i, 1])
            drain(cotb.at[:, 0], cot_send.at[i])

    @pl.when(core == 0)
    def _():
        drain(acts.at[0], hid_send.at[0])

    @pl.when(core == 1)
    def _():
        drain(acts.at[1, mine], hid_send.at[0])
        drain(acts.at[1, mine], hid_send.at[1])

    drain(acts.at[1, mine], hid_send.at[2])
    drain(packed.at[:, pl.ds(0, NZ - 1)], z_send)
    drain(result.at[:, pl.ds(0, SECTIONS - 1)], out_send)
    drain(result.at[:, pl.ds(0, 1)], out_own)
    drain(result.at[:, pl.ds(0, SECTIONS - 1)], out_recv)


def local(cotangent, routes, gate_prob, hidden):
    tokens, model = cotangent.shape[1:]
    ff = hidden.shape[5]
    depth = hidden.shape[2] * hidden.shape[3] * hidden.shape[4]
    rows = ff // SECTIONS
    half = model // 2
    chunks = half // CHUNK
    dma = pltpu.SemaphoreType.DMA
    bf16 = jnp.bfloat16
    anywhere = pl.BlockSpec(memory_space=pl.ANY)
    result = pl.pallas_call(
        kernel,
        name="pair_grad",
        out_shape=jax.ShapeDtypeStruct((SECTIONS // 2, rows, model), bf16),
        in_specs=[anywhere] * 4,
        out_specs=anywhere,
        scratch_shapes=[
            pltpu.VMEM((chunks, 4, tokens, CHUNK), bf16),
            pltpu.VMEM((4, 2, tokens), jnp.int32),
            pltpu.VMEM((4, 2, tokens), jnp.float32),
            pltpu.VMEM((4, 2 * NZ * CAP, tokens), bf16),
            pltpu.VMEM((4, 2 * NZ * CAP, tokens), jnp.float32),
            pltpu.VMEM((chunks, NZ, 2, 2, 2 * CAP, CHUNK), bf16),
            pltpu.VMEM((chunks, 2, 2, NZ, 2 * CAP, CHUNK), bf16),
            pltpu.VMEM((2, depth, ff), bf16),
            pltpu.VMEM((ff, 2 * depth), bf16),
            pltpu.VMEM((chunks, SECTIONS, rows, CHUNK), bf16),
            dma((4, 2)), dma((4, 2)), dma((4,)), dma((chunks, 4)), dma((3,)), dma((3,)),
            dma, dma((chunks,)), dma((chunks,)), dma, dma, dma,
        ],
        compiler_params=pltpu.CompilerParams(collective_id=0, has_side_effects=True),
    )(
        cotangent[0],
        routes[0].T,
        gate_prob[0].T,
        hidden.reshape(depth, ff),
    )
    return result[:, None]


def solution(mesh):
    return jax.shard_map(
        local,
        mesh=mesh,
        in_specs=(
            P("section", "expert", None),
            P("section", "expert", None),
            P("section", "expert", None),
            P("section", "expert", None, None, None, None),
        ),
        out_specs=P(None, "expert", "section", None),
        check_vma=False,
    )
```

time: 585 us -> 131 us (0.22)
  blocking collectives: 253 us -> 0 us
  local copies, waits for them, and re-layouts: 226 us -> 6.29 us
  Pallas kernels: 0 us -> 125 us
  other arithmetic: 93 us -> 0 us
  matrix products: 9.71 us -> 0 us
    all_to_all x2 -> x0, blocking collectives: 253 us -> none  [the longest x1 149 us: local(): lax.all_to_all(part[None], 'section', split_axis=1, concat_axis=0, tiled=...]
    pallas_call x0 -> x1, Pallas kernels: none -> 125 us  [local(): pl.pallas_call(kernel, name='pair_grad', out_shape=jax.ShapeDtypeStruct((...]
    unnamed x1 -> x0, other arithmetic: 77.6 us -> none
    scatter x1 -> x0, local copies, waits for them, and re-layouts: 66.4 us -> none  [pack_block(): empty.at[flat].set(weighted.reshape(-1, width))]
    unnamed x14 -> x1, local copies, waits for them, and re-layouts: 71 us -> 6.29 us
    broadcast_in_dim x2 -> x0, local copies, waits for them, and re-layouts: 56.8 us -> none  [the longest x1 54.3 us: local(): part[None]]
    slice x1 -> x0, local copies, waits for them, and re-layouts: 15.5 us -> none  [pair_add(): upper = jnp.flip(pieces[half:], 0).astype(jnp.float32)]
    mul x5 -> x0, local copies, waits for them, and re-layouts: 11.8 us -> none  [the longest x3 11.6 us: pack_block(): prob_blk[:, :, None] * cot_blk[:, None, :].astype(jnp.float32)]
where the time goes in v1:
time: 131 us
  Pallas kernels  125 us (95%)
  local copies, waits for them, and re-layouts  6.29 us (5%)
    pallas_call x1, Pallas kernels, local(): pl.pallas_call(kernel, name='pair_grad', out_shape=jax.ShapeDtypeStruct((...  125 us
    unnamed x1, local copies, waits for them, and re-layouts  6.29 us

profile of v1, /device:TPU:1, one launch (start us, length us, event | category | flops | bytes accessed | tf_op | source)
XLA Modules:
  0.0 131.3 jit_solution(13601809464112346676)
XLA Ops:
  0.0 125.0 %pair_grad.1 = bf16[8,96,4096]{2,1,0:T(8,128)(2,1)} custom-call(bf16[128,4096]{1,0:T(8,128)(2,1)} %bitcast.13, s32[2,128]{1,0:T(2,128)} %bitcast.14, f32[2,128]{1,0:T(2,128)} %bitcast.15, bf16[512,1536]{1,0:T(8,128)(2,1)} %bitcast.12), custom_call_target="tpu_custom_call" | custom-call | tf_op jit(solution)/shard_map/pair_grad/pallas_call | solution.py:246
  125.0 6.3 %copy.7 = bf16[8,1,96,4096]{3,2,1,0:T(8,128)(2,1)} copy(bf16[8,1,96,4096]{3,2,1,0:T(8,128)(2,1)} %bitcast.11) | data formatting | bytes 12582912

commit v2 on v1

--- a/solution.py
+++ b/solution.py
@@ -14,7 +14,9 @@
 BLK = 64
 SECTIONS = 16
 AHEAD = 4
+VMEM_LIMIT = 60_500_000
 CHUNK = 256
+TAIL = ((0, 128), (128, 128))
 STEPS = (
     (0, 1, 0), (1, 0, 0), (0, 3, 1), (1, 2, 0), (0, 2, 0), (1, 1, 1), (0, 0, 1), (1, 3, 0),
     (0, 1, 1), (1, 0, 1), (0, 3, 0), (1, 2, 1), (0, 2, 1), (1, 1, 0), (1, 3, 1),
@@ -130,7 +132,7 @@
     def spread(a):
         return jnp.broadcast_to(a[:, None, :], (NZ, CAP, TOK)).reshape(NZ * CAP, TOK)
 
-    for q in range(4):
+    def choose(q):
         drain(rts.at[q], meta_recv.at[q, 0])
         drain(gts.at[q], meta_recv.at[q, 1])
         first = rts[q, 0:1, :] == named
@@ -146,24 +148,37 @@
             total = jnp.sum(jnp.where(mine, weight, 0.0), axis=1, keepdims=True)
             gain[q, b * TOK : (b + 1) * TOK, :] = jnp.broadcast_to(total, (TOK, TOK))
 
-    def pack(n):
-        for q in range(4):
+    def pack_part(n, sec):
+        for q in (2 * sec, 2 * sec + 1):
             drain(cotb.at[n, q], cot_recv.at[n, q])
             picked = jnp.dot(sel[q], cotb[n, q], preferred_element_type=jnp.float32)
             scale = jnp.concatenate([gain[q]] * (width // TOK), axis=1)
             slots = (picked * scale).astype(jnp.bfloat16).reshape(2, NZ, CAP, width)
             for b in range(2):
-                packed[n, :, q // 2, b, (q % 2) * CAP : (q % 2 + 1) * CAP, :] = slots[b]
+                packed[n, :, sec, b, (q % 2) * CAP : (q % 2 + 1) * CAP, :] = slots[b]
+
+    def ship(n, src, dst, recv, own):
         for i in Z_STEPS:
             to = (z + i) % NZ
-            remote(packed.at[n, to], arrived.at[n, :, :, z], z_send, z_recv.at[n], (s, to * 2 + y_lo))
-        pltpu.make_async_copy(packed.at[n, z], arrived.at[n, :, :, z], z_own.at[n]).start()
+            remote(src(to), dst, z_send, recv, (s, to * 2 + y_lo))
+        pltpu.make_async_copy(src(z), dst, own).start()
+
+    def pack(n):
+        for sec in range(2):
+            pack_part(n, sec)
+        ship(n, lambda to: packed.at[n, to], arrived.at[n, :, :, z], z_recv.at[n], z_own.at[n])
 
     def pack_step(n, carry):
         pack(n)
         return carry
 
-    lax.fori_loop(0, AHEAD, pack_step, 0)
+    for sec in range(2):
+        choose(2 * sec)
+        choose(2 * sec + 1)
+        pack_part(0, sec)
+        ship(0, lambda to: packed.at[0, to, sec], arrived.at[0, sec, :, z], z_recv.at[0], z_own.at[0])
+
+    lax.fori_loop(1, AHEAD, pack_step, 0)
 
     mine = pl.ds(pl.multiple_of(core * block, block), block)
     theirs = pl.ds(pl.multiple_of((1 - core) * block, block), block)
@@ -180,30 +195,53 @@
 
     lax.fori_loop(0, ff // 256, turn, 0)
 
-    def multiply(n, carry):
-        @pl.when(n + AHEAD < chunks)
+    last = chunks - 1
+
+    def multiply(n, lanes):
+        start, size = lanes
+
+        def rows_of(g, inner):
+            lhs = acts_t[pl.ds(pl.multiple_of(g * 4 * rows, 4 * rows), 4 * rows), :]
+            rhs = arrived[n, :, :, :, :, start : start + size].reshape(depth, size)
+            total = jnp.dot(lhs, rhs, preferred_element_type=jnp.float32)
+            result[n, pl.ds(g * 4, 4), :, start : start + size] = total.astype(jnp.bfloat16).reshape(4, rows, size)
+            return inner
+
+        lax.fori_loop(0, SECTIONS // 4, rows_of, 0)
+        first = pl.multiple_of(core * half + n * width + start, TOK)
+        place_out = out.at[pair, :, pl.ds(first, size)]
+        for step in STEPS:
+            to = section_at(step)
+            remote(result.at[n, to, :, start : start + size], place_out, out_send, out_recv, (to, e))
+        pltpu.make_async_copy(result.at[n, s, :, start : start + size], place_out, out_own).start()
+
+    def step_on(n, carry):
+        @pl.when(n + AHEAD < last)
         def _():
             pack(n + AHEAD)
 
+        @pl.when(n + AHEAD == last)
+        def _():
+            for sec in range(2):
+                pack_part(last, sec)
+            for h, (start, size) in enumerate(TAIL):
+                cols = slice(start, start + size)
+                ship(
+                    last, lambda to: packed.at[last, to, :, :, :, cols], arrived.at[last, :, :, z, :, cols],
+                    z_recv.at[last + h], z_own.at[last + h],
+                )
+
         drain(arrived.at[n, :, :, pl.ds(0, NZ - 1)], z_recv.at[n])
         drain(packed.at[n, 0], z_own.at[n])
-
-        def rows_of(g, inner):
-            lhs = acts_t[pl.ds(pl.multiple_of(g * 4 * rows, 4 * rows), 4 * rows), :]
-            rhs = arrived[n].reshape(depth, width)
-            total = jnp.dot(lhs, rhs, preferred_element_type=jnp.float32)
-            result[n, pl.ds(g * 4, 4)] = total.astype(jnp.bfloat16).reshape(4, rows, width)
-            return inner
-
-        lax.fori_loop(0, SECTIONS // 4, rows_of, 0)
-        place_out = out.at[pair, :, pl.ds(pl.multiple_of(core * half + n * width, width), width)]
-        for step in STEPS:
-            to = section_at(step)
-            remote(result.at[n, to], place_out, out_send, out_recv, (to, e))
-        pltpu.make_async_copy(result.at[n, s], place_out, out_own).start()
+        multiply(n, (0, width))
         return carry
 
-    lax.fori_loop(0, chunks, multiply, 0)
+    lax.fori_loop(0, last, step_on, 0)
+    for h, (start, size) in enumerate(TAIL):
+        cols = slice(start, start + size)
+        drain(arrived.at[last, :, :, pl.ds(0, NZ - 1), :, cols], z_recv.at[last + h])
+        drain(packed.at[last, 0, :, :, :, cols], z_own.at[last + h])
+        multiply(last, (start, size))
 
     for i in range(4):
         if i == 0:
@@ -246,9 +284,9 @@
     result = pl.pallas_call(
         kernel,
         name="pair_grad",
-        out_shape=jax.ShapeDtypeStruct((SECTIONS // 2, rows, model), bf16),
+        out_shape=pltpu.VMEM((SECTIONS // 2, rows, model), bf16),
         in_specs=[anywhere] * 4,
-        out_specs=anywhere,
+        out_specs=pl.BlockSpec(memory_space=pltpu.VMEM),
         scratch_shapes=[
             pltpu.VMEM((chunks, 4, tokens, CHUNK), bf16),
             pltpu.VMEM((4, 2, tokens), jnp.int32),
@@ -261,9 +299,9 @@
             pltpu.VMEM((ff, 2 * depth), bf16),
             pltpu.VMEM((chunks, SECTIONS, rows, CHUNK), bf16),
             dma((4, 2)), dma((4, 2)), dma((4,)), dma((chunks, 4)), dma((3,)), dma((3,)),
-            dma, dma((chunks,)), dma((chunks,)), dma, dma, dma,
+            dma, dma((chunks + 1,)), dma((chunks + 1,)), dma, dma, dma,
         ],
-        compiler_params=pltpu.CompilerParams(collective_id=0, has_side_effects=True),
+        compiler_params=pltpu.CompilerParams(collective_id=0, has_side_effects=True, vmem_limit_bytes=VMEM_LIMIT),
     )(
         cotangent[0],
         routes[0].T,

time: 131 us -> 126 us (0.962)
  local copies, waits for them, and re-layouts: 6.29 us -> 2.71 us
  Pallas kernels: 125 us -> 123 us
    unnamed x1, local copies, waits for them, and re-layouts: 6.29 us -> 2.71 us
    pallas_call x1, Pallas kernels: 125 us -> 123 us  [local(): pl.pallas_call(kernel, name='pair_grad', out_shape=pltpu.VMEM((SECTIONS /...]
where the time goes in v2:
time: 126 us
  Pallas kernels  123 us (98%)
  local copies, waits for them, and re-layouts  2.71 us (2%)
    pallas_call x1, Pallas kernels, local(): pl.pallas_call(kernel, name='pair_grad', out_shape=pltpu.VMEM((SECTIONS /...  123 us
    unnamed x1, local copies, waits for them, and re-layouts  2.71 us

profile of v2, /device:TPU:1, one launch (start us, length us, event | category | flops | bytes accessed | tf_op | source)
XLA Modules:
  0.0 125.8 jit_solution(10628065069576988785)
XLA Ops:
  0.0 123.0 %pair_grad.1 = bf16[8,96,4096]{2,1,0:T(8,128)(2,1)S(1)} custom-call(bf16[128,4096]{1,0:T(8,128)(2,1)} %bitcast.13, s32[2,128]{1,0:T(2,128)} %bitcast.14, f32[2,128]{1,0:T(2,128)} %bitcast.15, bf16[512,1536]{1,0:T(8,128)(2,1)} %bitcast.12), custom_call_target="tpu_custom_call" | custom-call | tf_op jit(solution)/shard_map/pair_grad/pallas_call | solution.py:284
  123.0 2.7 %copy.7 = bf16[8,1,96,4096]{3,2,1,0:T(8,128)(2,1)} copy(bf16[8,1,96,4096]{3,2,1,0:T(8,128)(2,1)S(1)} %bitcast.11) | data formatting | bytes 12582912

commit v3 on v2

--- a/solution.py
+++ b/solution.py
@@ -21,6 +21,8 @@
     (0, 1, 0), (1, 0, 0), (0, 3, 1), (1, 2, 0), (0, 2, 0), (1, 1, 1), (0, 0, 1), (1, 3, 0),
     (0, 1, 1), (1, 0, 1), (0, 3, 0), (1, 2, 1), (0, 2, 1), (1, 1, 0), (1, 3, 1),
 )
+X_STEPS = ((0, 1, 0), (0, 3, 1), (0, 2, 0), (0, 0, 1), (0, 1, 1), (0, 3, 0), (0, 2, 1))
+RELAYED = 6
 Z_STEPS = (4, 3, 5, 2, 6, 1, 7)
 
 
@@ -30,8 +32,9 @@
 
 def kernel(
     cot, routes, gates, hid, out,
-    cotb, rts, gts, sel, gain, packed, arrived, acts, acts_t, result,
-    meta_send, meta_recv, cot_send, cot_recv, hid_send, hid_recv, z_send, z_recv, z_own, out_send, out_recv, out_own,
+    cotb, rts, gts, sel, gain, packed, arrived, acts, acts_t, result, relay,
+    meta_send, meta_recv, cot_send, cot_recv, hid_send, hid_recv, z_send, z_recv, z_own,
+    y_send, y_recv, out_send, out_recv, out_own,
 ):
     chunks, _, _, width = cotb.shape
     ff = acts.shape[2]
@@ -44,7 +47,13 @@
     z, y_lo = e // 2, e % 2
     chip = s // 2
     base = 2 * chip * (1 - core) + (14 - 2 * chip) * core
-    pair = 2 * chip * (1 - chip // 4) + (15 - 2 * chip) * (chip // 4)
+
+    def pair_of(c):
+        return 2 * c * (1 - c // 4) + (15 - 2 * c) * (c // 4)
+
+    pair = pair_of(chip)
+    across = ((y_hi + 1) % 2) * 8 + s % 8
+    pair_across = pair_of(across // 2)
     other_e = z * 2 + 1 - y_lo
     partner = 2 * chip + 1 - core
     source = core * 2 + y_lo
@@ -52,6 +61,17 @@
     def section_at(step):
         a, b, c = step
         return ((y_hi + a) % 2) * 8 + ((x + b) % 4) * 2 + (core + c) % 2
+
+    def cut(n, h):
+        return cot.at[:, pl.ds(pl.multiple_of(h * half + n * width, width), width)]
+
+    @pl.when(core == 0)
+    def _():
+        pltpu.make_async_copy(routes, rts.at[source], meta_recv.at[source, 0]).start()
+        pltpu.make_async_copy(gates, gts.at[source], meta_recv.at[source, 1]).start()
+        for n in range(chunks):
+            pltpu.make_async_copy(cut(n, 0), cotb.at[n, source], cot_recv.at[n, source]).start()
+        pltpu.make_async_copy(hid, acts.at[0], hid_recv.at[0]).start()
 
     barrier = pltpu.get_barrier_semaphore()
     peers = [(section_at(step), e) for step in STEPS]
@@ -68,39 +88,27 @@
 
     targets = [(h, f, (base + h, z * 2 + (y_lo + f) % 2)) for h in range(2) for f in range(2)]
 
-    def each_target(to_other, to_self):
+    def each_target(send):
         for i, (h, f, device) in enumerate(targets):
             if i == 0:
-                @pl.when(core == 0)
-                def _():
-                    to_self(h)
-
                 @pl.when(core == 1)
                 def _():
-                    to_other(i, h, device)
+                    send(i, h, device)
             else:
-                to_other(i, h, device)
+                send(i, h, device)
 
     def send_meta(i, h, device):
         remote(routes, rts.at[source], meta_send.at[i, 0], meta_recv.at[source, 0], device)
         remote(gates, gts.at[source], meta_send.at[i, 1], meta_recv.at[source, 1], device)
 
-    def keep_meta(h):
-        pltpu.make_async_copy(routes, rts.at[source], meta_recv.at[source, 0]).start()
-        pltpu.make_async_copy(gates, gts.at[source], meta_recv.at[source, 1]).start()
-
     def send_rows(n):
-        def cut(h):
-            return cot.at[:, pl.ds(pl.multiple_of(h * half + n * width, width), width)]
-
         each_target(
             lambda i, h, device: remote(
-                cut(h), cotb.at[n, source], cot_send.at[i], cot_recv.at[n, source], device
-            ),
-            lambda h: pltpu.make_async_copy(cut(h), cotb.at[n, source], cot_recv.at[n, source]).start(),
+                cut(n, h), cotb.at[n, source], cot_send.at[i], cot_recv.at[n, source], device
+            )
         )
 
-    each_target(send_meta, keep_meta)
+    each_target(send_meta)
     send_rows(0)
     send_rows(1)
 
@@ -108,7 +116,6 @@
 
     @pl.when(core == 0)
     def _():
-        pltpu.make_async_copy(hid, acts.at[0], hid_recv.at[0]).start()
         remote(hid, acts.at[0], hid_send.at[0], hid_recv.at[0], (partner, e))
 
     @pl.when(core == 1)
@@ -126,7 +133,7 @@
     token = lax.broadcasted_iota(jnp.int32, (TOK, TOK), 1)
     row = lax.broadcasted_iota(jnp.int32, (TOK, TOK), 0)
     earlier = jnp.where((row < token) & ((row >> 6) == (token >> 6)), 1.0, 0.0).astype(jnp.bfloat16)
-    place = (row & (CAP - 1)).astype(jnp.float32)
+    slot = (row & (CAP - 1)).astype(jnp.float32)
     named = lax.broadcasted_iota(jnp.int32, (NZ, TOK), 0) * 2 + y_lo
 
     def spread(a):
@@ -140,7 +147,7 @@
         hits = jnp.where(first | second, 1.0, 0.0)
         weight = jnp.where(first, gts[q, 0:1, :], 0.0) + jnp.where(second, gts[q, 1:2, :], 0.0)
         before = jnp.dot(hits.astype(jnp.bfloat16), earlier, preferred_element_type=jnp.float32)
-        chosen = (spread(hits) > 0.5) & (spread(before) == place)
+        chosen = (spread(hits) > 0.5) & (spread(before) == slot)
         weight = spread(weight)
         for b in range(2):
             mine = chosen & ((token >> 6) == b)
@@ -148,14 +155,21 @@
             total = jnp.sum(jnp.where(mine, weight, 0.0), axis=1, keepdims=True)
             gain[q, b * TOK : (b + 1) * TOK, :] = jnp.broadcast_to(total, (TOK, TOK))
 
+    def pack_rows(n, sec, j):
+        q = 2 * sec + j
+        drain(cotb.at[n, q], cot_recv.at[n, q])
+        picked = jnp.dot(sel[q], cotb[n, q], preferred_element_type=jnp.float32)
+        scale = jnp.concatenate([gain[q]] * (width // TOK), axis=1)
+        slots = (picked * scale).astype(jnp.bfloat16).reshape(2, NZ, CAP, width)
+        for b in range(2):
+            packed[n, :, sec, b, slots_of(j), :] = slots[b]
+
+    def slots_of(j):
+        return pl.ds(pl.multiple_of(j * CAP, CAP), CAP)
+
     def pack_part(n, sec):
-        for q in (2 * sec, 2 * sec + 1):
-            drain(cotb.at[n, q], cot_recv.at[n, q])
-            picked = jnp.dot(sel[q], cotb[n, q], preferred_element_type=jnp.float32)
-            scale = jnp.concatenate([gain[q]] * (width // TOK), axis=1)
-            slots = (picked * scale).astype(jnp.bfloat16).reshape(2, NZ, CAP, width)
-            for b in range(2):
-                packed[n, :, sec, b, (q % 2) * CAP : (q % 2 + 1) * CAP, :] = slots[b]
+        for j in range(2):
+            pack_rows(n, sec, j)
 
     def ship(n, src, dst, recv, own):
         for i in Z_STEPS:
@@ -172,11 +186,13 @@
         pack(n)
         return carry
 
-    for sec in range(2):
-        choose(2 * sec)
-        choose(2 * sec + 1)
-        pack_part(0, sec)
-        ship(0, lambda to: packed.at[0, to, sec], arrived.at[0, sec, :, z], z_recv.at[0], z_own.at[0])
+    for sec, j in ((0, y_lo), (0, 1 - y_lo), (1, 1 - y_lo), (1, y_lo)):
+        choose(2 * sec + j)
+        pack_rows(0, sec, j)
+        ship(
+            0, lambda to: packed.at[0, to, sec, :, slots_of(j)], arrived.at[0, sec, :, z, slots_of(j)],
+            z_recv.at[0], z_own.at[0],
+        )
 
     lax.fori_loop(1, AHEAD, pack_step, 0)
 
@@ -197,6 +213,10 @@
 
     last = chunks - 1
 
+    def place(p, n, lanes):
+        start, size = lanes
+        return out.at[p, :, pl.ds(pl.multiple_of(core * half + n * width + start, TOK), size)]
+
     def multiply(n, lanes):
         start, size = lanes
 
@@ -208,12 +228,29 @@
             return inner
 
         lax.fori_loop(0, SECTIONS // 4, rows_of, 0)
-        first = pl.multiple_of(core * half + n * width + start, TOK)
-        place_out = out.at[pair, :, pl.ds(first, size)]
+
+    def send_all(n, lanes):
+        start, size = lanes
         for step in STEPS:
             to = section_at(step)
-            remote(result.at[n, to, :, start : start + size], place_out, out_send, out_recv, (to, e))
-        pltpu.make_async_copy(result.at[n, s, :, start : start + size], place_out, out_own).start()
+            remote(result.at[n, to, :, start : start + size], place(pair, n, lanes), out_send.at[0], out_recv.at[0], (to, e))
+        pltpu.make_async_copy(result.at[n, s, :, start : start + size], place(pair, n, lanes), out_own.at[0]).start()
+
+    def send_near(n, lanes):
+        remote(result.at[n, pl.ds(((y_hi + 1) % 2) * 8, 8)], relay.at[n], y_send, y_recv.at[n], (across, e))
+        for step in X_STEPS:
+            to = section_at(step)
+            remote(result.at[n, to], place(pair, n, lanes), out_send.at[1], out_recv.at[1], (to, e))
+        pltpu.make_async_copy(result.at[n, s], place(pair, n, lanes), out_own.at[0]).start()
+
+    def pass_on(n, lanes):
+        drain(relay.at[n], y_recv.at[n])
+        for step in X_STEPS:
+            to = section_at(step)
+            remote(relay.at[n, to % 8], place(pair_across, n, lanes), out_send.at[2], out_recv.at[2], (to, e))
+        pltpu.make_async_copy(relay.at[n, s % 8], place(pair_across, n, lanes), out_own.at[1]).start()
+
+    full = (0, width)
 
     def step_on(n, carry):
         @pl.when(n + AHEAD < last)
@@ -233,7 +270,20 @@
 
         drain(arrived.at[n, :, :, pl.ds(0, NZ - 1)], z_recv.at[n])
         drain(packed.at[n, 0], z_own.at[n])
-        multiply(n, (0, width))
+        multiply(n, full)
+
+        @pl.when(n < RELAYED)
+        def _():
+            send_near(n, full)
+
+        @pl.when(n >= RELAYED)
+        def _():
+            send_all(n, full)
+
+        @pl.when((n >= 1) & (n <= RELAYED))
+        def _():
+            pass_on(n - 1, full)
+
         return carry
 
     lax.fori_loop(0, last, step_on, 0)
@@ -242,6 +292,7 @@
         drain(arrived.at[last, :, :, pl.ds(0, NZ - 1), :, cols], z_recv.at[last + h])
         drain(packed.at[last, 0, :, :, :, cols], z_own.at[last + h])
         multiply(last, (start, size))
+        send_all(last, (start, size))
 
     for i in range(4):
         if i == 0:
@@ -266,9 +317,15 @@
 
     drain(acts.at[1, mine], hid_send.at[2])
     drain(packed.at[:, pl.ds(0, NZ - 1)], z_send)
-    drain(result.at[:, pl.ds(0, SECTIONS - 1)], out_send)
-    drain(result.at[:, pl.ds(0, 1)], out_own)
-    drain(result.at[:, pl.ds(0, SECTIONS - 1)], out_recv)
+    direct = result.at[pl.ds(RELAYED, chunks - RELAYED), pl.ds(0, SECTIONS - 1)]
+    near = result.at[pl.ds(0, RELAYED), pl.ds(0, len(X_STEPS))]
+    drain(relay, y_send)
+    for sems in (out_send, out_recv):
+        drain(direct, sems.at[0])
+        drain(near, sems.at[1])
+        drain(near, sems.at[2])
+    drain(result.at[:, pl.ds(0, 1)], out_own.at[0])
+    drain(relay.at[:, pl.ds(0, 1)], out_own.at[1])
 
 
 def local(cotangent, routes, gate_prob, hidden):
@@ -298,8 +355,10 @@
             pltpu.VMEM((2, depth, ff), bf16),
             pltpu.VMEM((ff, 2 * depth), bf16),
             pltpu.VMEM((chunks, SECTIONS, rows, CHUNK), bf16),
+            pltpu.VMEM((RELAYED, SECTIONS // 2, rows, CHUNK), bf16),
             dma((4, 2)), dma((4, 2)), dma((4,)), dma((chunks, 4)), dma((3,)), dma((3,)),
-            dma, dma((chunks + 1,)), dma((chunks + 1,)), dma, dma, dma,
+            dma, dma((chunks + 1,)), dma((chunks + 1,)),
+            dma, dma((RELAYED,)), dma((3,)), dma((3,)), dma((2,)),
         ],
         compiler_params=pltpu.CompilerParams(collective_id=0, has_side_effects=True, vmem_limit_bytes=VMEM_LIMIT),
     )(

time: 126 us -> 130 us (1.032)
  Pallas kernels: 123 us -> 127 us
    pallas_call x1, Pallas kernels: 123 us -> 127 us  [local(): pl.pallas_call(kernel, name='pair_grad', out_shape=pltpu.VMEM((SECTIONS /...]
where the time goes in v3:
time: 130 us
  Pallas kernels  127 us (98%)
  local copies, waits for them, and re-layouts  2.71 us (2%)
    pallas_call x1, Pallas kernels, local(): pl.pallas_call(kernel, name='pair_grad', out_shape=pltpu.VMEM((SECTIONS /...  127 us
    unnamed x1, local copies, waits for them, and re-layouts  2.71 us

profile of v3, /device:TPU:1, one launch (start us, length us, event | category | flops | bytes accessed | tf_op | source)
XLA Modules:
  0.0 130.1 jit_solution(11192225588419306765)
XLA Ops:
  0.0 127.4 %pair_grad.1 = bf16[8,96,4096]{2,1,0:T(8,128)(2,1)S(1)} custom-call(bf16[128,4096]{1,0:T(8,128)(2,1)} %bitcast.13, s32[2,128]{1,0:T(2,128)} %bitcast.14, f32[2,128]{1,0:T(2,128)} %bitcast.15, bf16[512,1536]{1,0:T(8,128)(2,1)} %bitcast.12), custom_call_target="tpu_custom_call" | custom-call | tf_op jit(solution)/shard_map/pair_grad/pallas_call | solution.py:341
  127.4 2.7 %copy.7 = bf16[8,1,96,4096]{3,2,1,0:T(8,128)(2,1)} copy(bf16[8,1,96,4096]{3,2,1,0:T(8,128)(2,1)S(1)} %bitcast.11) | data formatting | bytes 12582912

commit v4 on v2

--- a/solution.py
+++ b/solution.py
@@ -16,6 +16,7 @@
 AHEAD = 4
 VMEM_LIMIT = 60_500_000
 CHUNK = 256
+EARLY = 4
 TAIL = ((0, 128), (128, 128))
 STEPS = (
     (0, 1, 0), (1, 0, 0), (0, 3, 1), (1, 2, 0), (0, 2, 0), (1, 1, 1), (0, 0, 1), (1, 3, 0),
@@ -101,8 +102,11 @@
         )
 
     each_target(send_meta, keep_meta)
-    send_rows(0)
-    send_rows(1)
+    def rest(n, carry):
+        send_rows(n)
+        return carry
+
+    lax.fori_loop(0, EARLY, rest, 0)
 
     block = acts.shape[1] // 2
 
@@ -117,11 +121,7 @@
             part = pl.ds(b * block, block)
             remote(hid.at[part], acts.at[1, part], hid_send.at[b], hid_recv.at[1], (base + b, e))
 
-    def rest(n, carry):
-        send_rows(n)
-        return carry
-
-    lax.fori_loop(2, chunks, rest, 0)
+    lax.fori_loop(EARLY, chunks, rest, 0)
 
     token = lax.broadcasted_iota(jnp.int32, (TOK, TOK), 1)
     row = lax.broadcasted_iota(jnp.int32, (TOK, TOK), 0)

time: 126 us -> 125 us (level)
  no operation moved by 1% of the time
where the time goes in v4:
time: 125 us
  Pallas kernels  122 us (98%)
  local copies, waits for them, and re-layouts  2.71 us (2%)
    pallas_call x1, Pallas kernels, local(): pl.pallas_call(kernel, name='pair_grad', out_shape=pltpu.VMEM((SECTIONS /...  122 us
    unnamed x1, local copies, waits for them, and re-layouts  2.71 us

profile of v4, /device:TPU:1, one launch (start us, length us, event | category | flops | bytes accessed | tf_op | source)
XLA Modules:
  0.0 124.6 jit_solution(10891862657965470660)
XLA Ops:
  0.0 121.9 %pair_grad.1 = bf16[8,96,4096]{2,1,0:T(8,128)(2,1)S(1)} custom-call(bf16[128,4096]{1,0:T(8,128)(2,1)} %bitcast.13, s32[2,128]{1,0:T(2,128)} %bitcast.14, f32[2,128]{1,0:T(2,128)} %bitcast.15, bf16[512,1536]{1,0:T(8,128)(2,1)} %bitcast.12), custom_call_target="tpu_custom_call" | custom-call | tf_op jit(solution)/shard_map/pair_grad/pallas_call | solution.py:284
  121.9 2.7 %copy.7 = bf16[8,1,96,4096]{3,2,1,0:T(8,128)(2,1)} copy(bf16[8,1,96,4096]{3,2,1,0:T(8,128)(2,1)S(1)} %bitcast.11) | data formatting | bytes 12582912

commit v5 on v4

--- a/solution.py
+++ b/solution.py
@@ -13,10 +13,10 @@
 TOK = 128
 BLK = 64
 SECTIONS = 16
-AHEAD = 4
+AHEAD = 5
 VMEM_LIMIT = 60_500_000
 CHUNK = 256
-EARLY = 4
+EARLY = 5
 TAIL = ((0, 128), (128, 128))
 STEPS = (
     (0, 1, 0), (1, 0, 0), (0, 3, 1), (1, 2, 0), (0, 2, 0), (1, 1, 1), (0, 0, 1), (1, 3, 0),

time: 125 us -> 125 us (level)
  no operation moved by 1% of the time
where the time goes in v5:
time: 125 us
  Pallas kernels  122 us (98%)
  local copies, waits for them, and re-layouts  2.71 us (2%)
    pallas_call x1, Pallas kernels, local(): pl.pallas_call(kernel, name='pair_grad', out_shape=pltpu.VMEM((SECTIONS /...  122 us
    unnamed x1, local copies, waits for them, and re-layouts  2.71 us

profile of v5, /device:TPU:1, one launch (start us, length us, event | category | flops | bytes accessed | tf_op | source)
XLA Modules:
  0.0 124.7 jit_solution(11709451470524403841)
XLA Ops:
  0.0 122.0 %pair_grad.1 = bf16[8,96,4096]{2,1,0:T(8,128)(2,1)S(1)} custom-call(bf16[128,4096]{1,0:T(8,128)(2,1)} %bitcast.13, s32[2,128]{1,0:T(2,128)} %bitcast.14, f32[2,128]{1,0:T(2,128)} %bitcast.15, bf16[512,1536]{1,0:T(8,128)(2,1)} %bitcast.12), custom_call_target="tpu_custom_call" | custom-call | tf_op jit(solution)/shard_map/pair_grad/pallas_call | solution.py:284
  122.0 2.7 %copy.7 = bf16[8,1,96,4096]{3,2,1,0:T(8,128)(2,1)} copy(bf16[8,1,96,4096]{3,2,1,0:T(8,128)(2,1)S(1)} %bitcast.11) | data formatting | bytes 12582912
